TPU v7x, 256 devices: a whole 4x4x8 slice. The times are simulated.
256 devices in a mesh: src: 32 (over z, y), tgt: 8 (over x, core).
Axes of the slice: x: 4, y: 4, z: 8, core: 2. Of those that a mesh axis runs over, the one named last changes fastest.
Arguments:
- source: bfloat16 [32768, 300], P('src'), may hold values from -70 to 70
- target: bfloat16 [16384, 300], P('tgt'), may hold values from -11 to 11
- start_map: float32 [300, 300], replicated, may hold values from -1.5 to 1.5
Outputs:
- source_soft: bfloat16 [32768, 300], P(('src', 'tgt'))
- target_soft: bfloat16 [16384, 300], P('tgt')
- polar_map: float32 [300, 300], replicated
All inputs are finite; a program needn't handle non-finite values.
Results may differ from a plain program's by a relative error of at most 0.014.
The roundings to bfloat16 on the way count: a program that leaves them out, or rounds other values in their place, can miss the bound.
Values may be sent and summed in bfloat16 or wider, within the bound.
A program may use at most 64 MiB of HBM per device.

v0:
```python
import math
import jax
import jax.numpy as jnp
from jax import lax
from jax.sharding import PartitionSpec as P

ITERS = 2
NEWTON_STEPS = 8


def polar_steps(covariance):
    highest = lax.Precision.HIGHEST
    current = covariance / jnp.sqrt(jnp.sum(covariance * covariance) + 1e-06)
    for newton in range(NEWTON_STEPS):
        gram_matrix = jnp.dot(current.T, current, precision=highest)
        current = 1.5 * current - 0.5 * jnp.dot(current, gram_matrix, precision=highest)
    return current


def translation_sums(row_weights, col_weights, source, target, share_target, src_index):
    source_sum = lax.psum_scatter(
        jnp.dot(row_weights, target, preferred_element_type=jnp.float32),
        "tgt",
        scatter_dimension=0,
        tiled=True,
    )
    target_full = lax.psum(
        lax.dot_general(
            col_weights, source, (((0,), (0,)), ((), ())), preferred_element_type=jnp.float32
        ),
        "src",
    )
    target_sum = lax.dynamic_slice_in_dim(target_full, src_index * share_target, share_target, 0)
    return (source_sum, target_sum, target_full)


def body(source, target, start_map):
    highest = lax.Precision.HIGHEST
    score_scale = 2.0 / math.sqrt(source.shape[1])
    rows_source = source.shape[0]
    rows_target = target.shape[0]
    src_devices = lax.axis_size("src")
    tgt_devices = lax.axis_size("tgt")
    src_index = lax.axis_index("src")
    tgt_index = lax.axis_index("tgt")
    share_source = rows_source // tgt_devices
    share_target = rows_target // src_devices
    source_piece = lax.dynamic_slice_in_dim(
        source, tgt_index * share_source, share_source, 0
    ).astype(jnp.float32)
    target_piece = lax.dynamic_slice_in_dim(
        target, src_index * share_target, share_target, 0
    ).astype(jnp.float32)
    current = start_map
    source_sum = None
    target_sum = None
    target_full = None
    for iteration in range(ITERS):
        mapped = jnp.dot(
            source, current.astype(jnp.bfloat16), preferred_element_type=jnp.float32
        ).astype(jnp.bfloat16)
        scores = (
            lax.dot_general(
                mapped, target, (((1,), (1,)), ((), ())), preferred_element_type=jnp.float32
            )
            * score_scale
        )
        row_local = jnp.max(scores, axis=1)
        col_local = jnp.max(scores, axis=0)
        row_top = lax.pmax(row_local, "tgt")
        col_top = lax.pmax(col_local, "src")
        row_total = lax.psum(jnp.sum(jnp.exp(scores - row_top[:, None]), axis=1), "tgt")
        col_total = lax.psum(jnp.sum(jnp.exp(scores - col_top[None, :]), axis=0), "src")
        row_weights = (jnp.exp(scores - row_top[:, None]) / row_total[:, None]).astype(jnp.bfloat16)
        col_weights = (jnp.exp(scores - col_top[None, :]) / col_total[None, :]).astype(jnp.bfloat16)
        source_sum, target_sum, target_full = translation_sums(
            row_weights, col_weights, source, target, share_target, src_index
        )
        covariance = jnp.dot(source_piece.T, source_sum, precision=highest)
        covariance = covariance + jnp.dot(target_sum.T, target_piece, precision=highest)
        covariance = lax.psum(covariance, ("src", "tgt"))
        current = polar_steps(covariance)
    source_share = source_sum.astype(jnp.bfloat16)
    target_soft = target_full.astype(jnp.bfloat16)
    return (source_share, target_soft, current)


def solution(mesh):
    in_specs = (P("src", None), P("tgt", None), P())
    out_specs = (P(("src", "tgt"), None), P("tgt", None), P())
    return jax.shard_map(body, mesh=mesh, in_specs=in_specs, out_specs=out_specs, check_vma=False)
```

profile of v0, /device:TPU:2, one launch (start us, length us, event | category | flops | bytes accessed | tf_op | source)
XLA Modules:
  0.0 1263.8 jit_solution(214851185553863919)
XLA Ops:
  9.3 7.3 multiply_reduce_fusion.2
  16.6 78.9 %pmax.29 = f32[2048]{0:T(1024)S(1)} all-reduce(f32[2048]{0:T(1024)S(1)} %get-tuple-element.9), channel_id=1, replica_groups=mesh['src'=32,'tgt'=8] {'src'}, use_global_device_ids=true, to_apply=%region_6.0 | all-reduce | flops 2048 | bytes 16384 | tf_op jit(solution)/shard_map/pmax | solution.py:71
  95.5 10.0 pmax.28
  105.6 5.2 fusion.1
  110.8 12.4 psum.56
  123.2 7.0 fusion.6
  130.3 70.6 %psum.57 = f32[2048]{0:T(1024)S(1)} all-reduce(f32[2048]{0:T(1024)S(1)} %get-tuple-element.7), channel_id=1, replica_groups=mesh['src'=32,'tgt'=8] {'src'}, use_global_device_ids=true, to_apply=%region_8.0 | all-reduce | flops 2048 | bytes 16384 | tf_op jit(solution)/shard_map/psum | solution.py:73
  201.0 7.6 fusion.4
  210.0 153.4 %all-reduce.5.cloned.1.call-done = f32[2048,300]{1,0:T(8,128)} async-done(((f32[2048,300]{1,0:T(8,128)}), f32[2048,300]{1,0:T(8,128)}) %all-reduce.5.cloned.1.call-update) | async-done | bytes 2457616 | tf_op jit(solution)/shard_map/psum | solution.py:27
  365.8 248.9 %all-reduce.7.cloned.1.call-done = f32[300,300]{1,0:T(8,128)} async-done(((f32[300,300]{1,0:T(8,128)}), f32[300,300]{1,0:T(8,128)}) %all-reduce.7.cloned.1.call-update) | async-done | bytes 360016 | tf_op jit(solution)/shard_map/psum | solution.py:81
  617.1 2.4 fusion.29
  638.2 5.3 multiply_reduce_fusion
  643.5 72.1 %pmax.31 = f32[2048]{0:T(1024)S(1)} all-reduce(f32[2048]{0:T(1024)S(1)} %get-tuple-element.5), channel_id=1, replica_groups=mesh['src'=32,'tgt'=8] {'src'}, use_global_device_ids=true, to_apply=%region_18.0 | all-reduce | flops 2048 | bytes 16384 | tf_op jit(solution)/shard_map/pmax | solution.py:71
  715.6 10.0 pmax.30
  725.6 5.2 fusion.3
  730.9 12.6 %psum.60 = f32[1024]{0:T(1024)S(1)} all-reduce(f32[1024]{0:T(1024)S(1)} %get-tuple-element.4), channel_id=1, replica_groups=mesh['src'=32,'tgt'=8] {'tgt'}, use_global_device_ids=true, to_apply=%region_15.0 | all-reduce | flops 1024 | bytes 8192 | tf_op jit(solution)/shard_map/psum | solution.py:72
  743.5 6.4 fusion.7
  750.0 70.8 %psum.61 = f32[2048]{0:T(1024)S(1)} all-reduce(f32[2048]{0:T(1024)S(1)} %get-tuple-element.3), channel_id=1, replica_groups=mesh['src'=32,'tgt'=8] {'src'}, use_global_device_ids=true, to_apply=%region_20.0 | all-reduce | flops 2048 | bytes 16384 | tf_op jit(solution)/shard_map/psum | solution.py:73
  820.8 6.8 fusion.5
  829.2 151.9 %all-reduce.9.cloned.1.call-done = f32[2048,300]{0,1:T(8,128)} async-done(((f32[2048,300]{0,1:T(8,128)}), f32[2048,300]{0,1:T(8,128)}) %all-reduce.9.cloned.1.call-update) | async-done | bytes 2457616 | tf_op jit(solution)/shard_map/psum | solution.py:27
  984.8 2.9 convert_element_type.42
  987.7 244.7 %all-reduce.11.cloned.1.call-done = f32[300,300]{1,0:T(8,128)} async-done(((f32[300,300]{1,0:T(8,128)}), f32[300,300]{1,0:T(8,128)}) %all-reduce.11.cloned.1.call-update) | async-done | bytes 360016 | tf_op jit(solution)/shard_map/psum | solution.py:81
  1234.8 2.4 fusion.30
  1237.2 2.2 fusion.17
  (54 shorter events, 49.3 us)
Async XLA Ops:
  8.0 1.3 copy-start
  8.0 200.7 %reduce-scatter.3.cloned.1.call-start = ((), (), s32[]{:S(2)}) async-start(), calls=%async_computation.2 | async-start | bytes 1769472 | tf_op jit(solution)/shard_map/reduce_scatter | solution.py:21
  123.2 77.8 %copy-start.1 = (bf16[1024,300]{0,1:T(8,128)(2,1)S(1)}, bf16[1024,300]{0,1:T(8,128)(2,1)}, u32[]{:S(2)}) copy-start(bf16[1024,300]{0,1:T(8,128)(2,1)} %param.3) | copy-start | bytes 1843204
  130.3 233.1 %all-reduce.5.cloned.1.call-start = ((), (), s32[]{:S(2)}) async-start(), calls=%async_computation.3 | async-start | bytes 6291456 | tf_op jit(solution)/shard_map/psum | solution.py:27
  208.6 406.1 %all-reduce.7.cloned.1.call-start = ((), (), s32[]{:S(2)}) async-start(), calls=%async_computation.4 | async-start | bytes 933888 | tf_op jit(solution)/shard_map/psum | solution.py:81
  365.5 462.4 %reduce-scatter.5.cloned.1.call-start = ((), (), s32[]{:S(2)}) async-start(), calls=%async_computation.5 | async-start | bytes 1400832 | tf_op jit(solution)/shard_map/reduce_scatter | solution.py:21
  749.9 231.1 %all-reduce.9.cloned.1.call-start = ((), (), s32[]{:S(2)}) async-start(), calls=%async_computation.6 | async-start | bytes 4980736 | tf_op jit(solution)/shard_map/psum | solution.py:27
  827.7 404.7 %all-reduce.11.cloned.1.call-start = ((), (), s32[]{:S(2)}) async-start(), calls=%async_computation.7 | async-start | bytes 933888 | tf_op jit(solution)/shard_map/psum | solution.py:81
Sparse Core Ops, SparseCore 0:
  130.4 26.5 reduce-scatter.2
  365.6 248.9 all-reduce.6
  750.1 27.8 reduce-scatter.4
  983.3 249.0 all-reduce.10
Sparse Core Ops, SparseCore 1:
  208.7 154.6 all-reduce.4
  827.8 153.2 all-reduce.8
where the time goes:
time: 1270 us; the launch traced here: 1260 us
  waiting for transfers between devices  799 us (63%)
  blocking collectives  338 us (27%)
  matrix products  89.8 us (7%)
  other arithmetic  18.4 us (1%)
  between operations  17.2 us (1%)
    psum x2, waiting for transfers between devices, body(): covariance = lax.psum(covariance, ('src', 'tgt'))  494 us
    psum x2, waiting for transfers between devices, translation_sums(): lax.psum(lax.dot_general(col_weights, source, (((0,), (0,)), ((), ())), p...  305 us
    pmax x2, blocking collectives, body(): col_top = lax.pmax(col_local, 'src')  151 us
    psum x2, blocking collectives, body(): lax.psum(jnp.sum(jnp.exp(scores - col_top[None, :]), axis=0), 'src')  141 us
  transfers between devices with their start and end apart: 6, of which 4 were waited for; matrix products, arithmetic and copies ran while one was open for 2% of the time, Pallas kernels for 0%

commit v1 on v0

--- a/solution.py
+++ b/solution.py
@@ -78,7 +78,8 @@
         )
         covariance = jnp.dot(source_piece.T, source_sum, precision=highest)
         covariance = covariance + jnp.dot(target_sum.T, target_piece, precision=highest)
-        covariance = lax.psum(covariance, ("src", "tgt"))
+        partial = lax.psum(covariance, "src")
+        covariance = lax.psum(partial, "tgt")
         current = polar_steps(covariance)
     source_share = source_sum.astype(jnp.bfloat16)
     target_soft = target_full.astype(jnp.bfloat16)

time: 1270 us -> 1210 us (0.953)
  waiting for transfers between devices: 799 us -> 714 us
    psum x2 -> x4, waiting for transfers between devices: 494 us -> 408 us  [the longest x2 292 us: body(): partial = lax.psum(covariance, 'src')]
  transfers between devices with their start and end apart: 6 -> 8, of which waited for: 4 -> 6; matrix products, arithmetic and copies ran while one was open for 2% -> 2% of each run, Pallas kernels for 0% -> 0%
where the time goes in v1:
time: 1210 us; the launch traced here: 1200 us
  waiting for transfers between devices  714 us (59%)
  blocking collectives  344 us (28%)
  matrix products  99.5 us (8%)
  other arithmetic  18.4 us (2%)
  between operations  17.7 us (1%)
    psum x2, waiting for transfers between devices, translation_sums(): lax.psum(lax.dot_general(col_weights, source, (((0,), (0,)), ((), ())), p...  305 us
    psum x2, waiting for transfers between devices, body(): partial = lax.psum(covariance, 'src')  292 us
    pmax x2, blocking collectives, body(): col_top = lax.pmax(col_local, 'src')  155 us
    psum x2, blocking collectives, body(): lax.psum(jnp.sum(jnp.exp(scores - col_top[None, :]), axis=0), 'src')  141 us
    psum x2, waiting for transfers between devices, body(): covariance = lax.psum(partial, 'tgt')  116 us
    dot_general x16, matrix products, polar_steps(): gram_matrix = jnp.dot(current.T, current, precision=highest)  32.4 us
    psum x2, blocking collectives, body(): lax.psum(jnp.sum(jnp.exp(scores - row_top[:, None]), axis=1), 'tgt')  25.3 us
  transfers between devices with their start and end apart: 8, of which 6 were waited for; matrix products, arithmetic and copies ran while one was open for 2% of the time, Pallas kernels for 0%

profile of v1, /device:TPU:2, one launch (start us, length us, event | category | flops | bytes accessed | tf_op | source)
XLA Modules:
  0.0 1195.5 jit_solution(12933933521449382833)
XLA Ops:
  9.3 7.3 multiply_reduce_fusion.2
  16.6 78.9 %pmax.29 = f32[2048]{0:T(1024)S(1)} all-reduce(f32[2048]{0:T(1024)S(1)} %get-tuple-element.9), channel_id=1, replica_groups=mesh['src'=32,'tgt'=8] {'src'}, use_global_device_ids=true, to_apply=%region_6.0 | all-reduce | flops 2048 | bytes 16384 | tf_op jit(solution)/shard_map/pmax | solution.py:71
  95.5 10.0 pmax.28
  105.6 5.2 fusion.1
  110.8 12.4 %psum.70 = f32[1024]{0:T(1024)S(1)} all-reduce(f32[1024]{0:T(1024)S(1)} %get-tuple-element.8), channel_id=1, replica_groups=mesh['src'=32,'tgt'=8] {'tgt'}, use_global_device_ids=true, to_apply=%region_3.0 | all-reduce | flops 1024 | bytes 8192 | tf_op jit(solution)/shard_map/psum | solution.py:72
  123.2 7.0 fusion.6
  130.3 70.6 %psum.71 = f32[2048]{0:T(1024)S(1)} all-reduce(f32[2048]{0:T(1024)S(1)} %get-tuple-element.7), channel_id=1, replica_groups=mesh['src'=32,'tgt'=8] {'src'}, use_global_device_ids=true, to_apply=%region_8.0 | all-reduce | flops 2048 | bytes 16384 | tf_op jit(solution)/shard_map/psum | solution.py:73
  201.0 7.6 fusion.4
  210.0 153.3 %all-reduce.7.cloned.1.call-done = f32[2048,300]{1,0:T(8,128)} async-done(((f32[2048,300]{1,0:T(8,128)}), f32[2048,300]{1,0:T(8,128)}) %all-reduce.7.cloned.1.call-update) | async-done | bytes 2457616 | tf_op jit(solution)/shard_map/psum | solution.py:27
  365.5 146.2 %all-reduce.9.cloned.1.call-done = f32[300,300]{1,0:T(8,128)} async-done(((f32[300,300]{1,0:T(8,128)}), f32[300,300]{1,0:T(8,128)}) %all-reduce.9.cloned.1.call-update) | async-done | bytes 360016 | tf_op jit(solution)/shard_map/psum | solution.py:81
  512.0 60.0 %all-reduce.11.cloned.1.call-done = f32[300,300]{1,0:T(8,128)} async-done(((f32[300,300]{1,0:T(8,128)}), f32[300,300]{1,0:T(8,128)}) %all-reduce.11.cloned.1.call-update) | async-done | bytes 360016 | tf_op jit(solution)/shard_map/psum | solution.py:82
  588.3 11.2 fusion.53
  605.2 5.3 multiply_reduce_fusion
  610.5 76.1 %pmax.31 = f32[2048]{0:T(1024)S(1)} all-reduce(f32[2048]{0:T(1024)S(1)} %get-tuple-element.5), channel_id=1, replica_groups=mesh['src'=32,'tgt'=8] {'src'}, use_global_device_ids=true, to_apply=%region_19.0 | all-reduce | flops 2048 | bytes 16384 | tf_op jit(solution)/shard_map/pmax | solution.py:71
  686.6 12.3 %pmax.30 = f32[1024]{0:T(1024)S(1)} all-reduce(f32[1024]{0:T(1024)S(1)} %get-tuple-element.6), channel_id=1, replica_groups=mesh['src'=32,'tgt'=8] {'tgt'}, use_global_device_ids=true, to_apply=%region_14.0 | all-reduce | flops 1024 | bytes 8192 | tf_op jit(solution)/shard_map/pmax | solution.py:70
  698.9 5.2 fusion.3
  704.2 12.9 %psum.75 = f32[1024]{0:T(1024)S(1)} all-reduce(f32[1024]{0:T(1024)S(1)} %get-tuple-element.4), channel_id=1, replica_groups=mesh['src'=32,'tgt'=8] {'tgt'}, use_global_device_ids=true, to_apply=%region_16.0 | all-reduce | flops 1024 | bytes 8192 | tf_op jit(solution)/shard_map/psum | solution.py:72
  717.1 6.4 fusion.7
  723.6 70.6 %psum.76 = f32[2048]{0:T(1024)S(1)} all-reduce(f32[2048]{0:T(1024)S(1)} %get-tuple-element.3), channel_id=1, replica_groups=mesh['src'=32,'tgt'=8] {'src'}, use_global_device_ids=true, to_apply=%region_21.0 | all-reduce | flops 2048 | bytes 16384 | tf_op jit(solution)/shard_map/psum | solution.py:73
  794.3 6.8 fusion.5
  802.5 152.1 %all-reduce.13.cloned.1.call-done = f32[2048,300]{0,1:T(8,128)} async-done(((f32[2048,300]{0,1:T(8,128)}), f32[2048,300]{0,1:T(8,128)}) %all-reduce.13.cloned.1.call-update) | async-done | bytes 2457616 | tf_op jit(solution)/shard_map/psum | solution.py:27
  957.0 146.3 %all-reduce.15.cloned.1.call-done = f32[300,300]{1,0:T(8,128)} async-done(((f32[300,300]{1,0:T(8,128)}), f32[300,300]{1,0:T(8,128)}) %all-reduce.15.cloned.1.call-update) | async-done | bytes 360016 | tf_op jit(solution)/shard_map/psum | solution.py:81
  1104.9 2.9 convert_element_type.42
  1107.8 55.8 %all-reduce.17.cloned.1.call-done = f32[300,300]{1,0:T(8,128)} async-done(((f32[300,300]{1,0:T(8,128)}), f32[300,300]{1,0:T(8,128)}) %all-reduce.17.cloned.1.call-update) | async-done | bytes 360016 | tf_op jit(solution)/shard_map/psum | solution.py:82
  (60 shorter events, 55.0 us)
Async XLA Ops:
  8.0 1.3 copy-start
  8.0 200.7 %reduce-scatter.3.cloned.1.call-start = ((), (), s32[]{:S(2)}) async-start(), calls=%async_computation.2 | async-start | bytes 1769472 | tf_op jit(solution)/shard_map/reduce_scatter | solution.py:21
  123.2 77.8 %copy-start.1 = (bf16[1024,300]{0,1:T(8,128)(2,1)S(1)}, bf16[1024,300]{0,1:T(8,128)(2,1)}, u32[]{:S(2)}) copy-start(bf16[1024,300]{0,1:T(8,128)(2,1)} %param.3) | copy-start | bytes 1843204
  130.3 233.0 %all-reduce.7.cloned.1.call-start = ((), (), s32[]{:S(2)}) async-start(), calls=%async_computation.3 | async-start | bytes 6291456 | tf_op jit(solution)/shard_map/psum | solution.py:27
  208.6 303.1 %all-reduce.9.cloned.1.call-start = ((), (), s32[]{:S(2)}) async-start(), calls=%async_computation.4 | async-start | bytes 933888 | tf_op jit(solution)/shard_map/psum | solution.py:81
  365.5 206.6 %all-reduce.11.cloned.1.call-start = ((), (), s32[]{:S(2)}) async-start(), calls=%async_computation.5 | async-start | bytes 933888 | tf_op jit(solution)/shard_map/psum | solution.py:82
  511.7 289.5 %reduce-scatter.5.cloned.1.call-start = ((), (), s32[]{:S(2)}) async-start(), calls=%async_computation.6 | async-start | bytes 1400832 | tf_op jit(solution)/shard_map/reduce_scatter | solution.py:21
  723.6 231.0 %all-reduce.13.cloned.1.call-start = ((), (), s32[]{:S(2)}) async-start(), calls=%async_computation.7 | async-start | bytes 4980736 | tf_op jit(solution)/shard_map/psum | solution.py:27
  801.1 302.1 %all-reduce.15.cloned.1.call-start = ((), (), s32[]{:S(2)}) async-start(), calls=%async_computation.8 | async-start | bytes 933888 | tf_op jit(solution)/shard_map/psum | solution.py:81
  956.7 206.9 %all-reduce.17.cloned.1.call-start = ((), (), s32[]{:S(2)}) async-start(), calls=%async_computation.9 | async-start | bytes 933888 | tf_op jit(solution)/shard_map/psum | solution.py:82
Sparse Core Ops, SparseCore 0:
  130.4 26.5 reduce-scatter.2
  511.8 60.1 all-reduce.10
  723.7 27.6 reduce-scatter.4
  1103.4 60.1 all-reduce.16
Sparse Core Ops, SparseCore 1:
  208.7 154.5 all-reduce.6
  367.5 144.2 all-reduce.8
  801.2 153.3 all-reduce.12
  958.9 144.3 all-reduce.14
